TPU v7x, 128 devices: a whole 4x4x4 slice. The times are simulated.
128 devices in a mesh: grp: 2 (over y_lo), sp: 64 (over x, y_hi, z, core).
Axes of the slice: x: 4, y: 4 (y_hi: 2, y_lo: 2; y = y_hi * 2 + y_lo), z: 4, core: 2. Of those that a mesh axis runs over, the one named last changes fastest.
Arguments:
- modes: bfloat16 [3, 512, 32, 16, 256], P(None, 'sp', 'grp'), may hold values from -16 to 16
- convecting: int32 [12], replicated, may hold values from 0 to 255, as said below
Outputs:
- skew_tensor: float32 [12, 256, 256], P(None, 'sp')
Inputs may be any that keep to these rules, and one draw needn't show every extreme that they name: `convecting`: 12 distinct mode indices.
All inputs are finite; a program needn't handle non-finite values.
Results may differ from a plain program's by a relative error of at most 0.0029.
Values may be sent and summed in bfloat16 or wider, within the bound.
No kernel may reach another device: no remote copies, remote signals or barrier semaphores. Data moves between devices by JAX's collectives and lax.ppermute only.
A program may use at most 64 MiB of HBM per device.

v0:
```python
import math

import jax
import jax.numpy as jnp
from jax import lax
from jax.sharding import PartitionSpec as P


def extended(block, sides, width):
    for axis, dim in sides:
        count = lax.axis_size(axis)
        forward = [(i, i + 1) for i in range(count - 1)]
        forward.append((count - 1, 0))
        backward = [(target, source) for source, target in forward]
        low = lax.ppermute(
            lax.slice_in_dim(block, block.shape[dim] - width, None, axis=dim), axis, forward
        )
        high = lax.ppermute(lax.slice_in_dim(block, 0, width, axis=dim), axis, backward)
        block = jnp.concatenate([low, block, high], axis=dim)
    return block


def shards(modes, convecting):
    n_sp = lax.axis_size("sp")
    n_grp = lax.axis_size("grp")
    width = modes.shape[4]
    cells = modes.shape[1] * n_sp * modes.shape[2] * n_grp * modes.shape[3]
    padded = extended(modes, (("grp", 2), ("sp", 1)), 1)
    picker = (jnp.arange(width, dtype=jnp.int32)[:, None] == convecting[None, :]).astype(
        jnp.bfloat16
    )
    velocity = jnp.einsum("cxyzm,ms->scxyz", modes, picker, preferred_element_type=jnp.float32)
    test_flat = modes.reshape(-1, width)

    def project(carry, field):
        centre = padded[:, 1:-1, 1:-1].astype(jnp.float32)
        along_x = padded[:, 2:, 1:-1].astype(jnp.float32) - padded[:, :-2, 1:-1].astype(jnp.float32)
        along_y = padded[:, 1:-1, 2:].astype(jnp.float32) - padded[:, 1:-1, :-2].astype(jnp.float32)
        along_z = jnp.roll(centre, -1, axis=3) - jnp.roll(centre, 1, axis=3)
        moved = 0.5 * (
            field[0][..., None] * along_x
            + field[1][..., None] * along_y
            + field[2][..., None] * along_z
        )
        moved = moved.astype(jnp.bfloat16).reshape(-1, width)
        block = lax.dot_general(
            test_flat, moved, (((0,), (0,)), ((), ())), preferred_element_type=jnp.float32
        )
        return (carry, block)

    _, stacked = lax.scan(project, jnp.zeros((), jnp.float32), velocity)
    mine = lax.psum_scatter(stacked, "sp", scatter_dimension=1, tiled=True)
    owned = lax.psum(mine, "grp")
    owned = owned / math.sqrt(cells)
    mirrored = lax.all_to_all(owned, "sp", split_axis=2, concat_axis=1, tiled=True)
    return 0.5 * (owned - jnp.swapaxes(mirrored, 1, 2))


def solution(mesh):
    placed = (P(None, "sp", "grp", None, None), P())
    return jax.shard_map(
        shards, mesh=mesh, in_specs=placed, out_specs=P(None, "sp", None), check_vma=False
    )
```

profile of v0, /device:TPU:0, one launch (start us, length us, event | category | flops | bytes accessed | tf_op | source)
XLA Modules:
  0.0 909.7 jit_solution(5108024089505814859)
XLA Ops:
  7.6 1.8 collective-permute-start
  9.7 5.7 collective-permute-done
  15.5 2.3 constant_dynamic-update-slice_fusion.2
  18.5 1.7 copy-done.1
  21.3 7.6 collective-permute-start.3
  28.9 5.6 fusion.6
  35.2 3.4 pad_maximum_fusion
  38.6 183.5 %while.10 = (s32[]{:T(128)}, f32[12,256,256]{2,1,0:T(8,128)}, f32[12,3,8,16,16]{4,0,3,2,1:T(8,128)}, bf16[3,10,18,16,256]{4,3,2,1,0:T(8,128)(2,1)}, bf16[3,8,18,...) while((s32[]{:T(128)}, f32[12,256,256]{2,1,0:T(8,128)}, ...), condition=%wide.region_1.2_spmd, body=%wide.region_0.1_spmd.sunk | while | flops 830472192 | bytes 61203032 | solution.py:51
  38.6 1.6 constant_dynamic-slice_fusion.3
  40.2 1.9 fusion.24
  42.9 7.4 fusion.25
  50.3 1.7 convolution_bitcast_fusion.2
  53.9 1.5 constant_dynamic-slice_fusion.3
  55.4 1.9 fusion.24
  58.2 7.4 fusion.25
  65.6 1.7 convolution_bitcast_fusion.2
  67.3 1.1 copy.35
  69.2 1.5 constant_dynamic-slice_fusion.3
  70.7 1.9 fusion.24
  73.5 7.4 fusion.25
  80.9 1.7 convolution_bitcast_fusion.2
  84.4 1.5 constant_dynamic-slice_fusion.3
  86.0 1.9 fusion.24
  88.8 7.4 fusion.25
  96.2 1.7 convolution_bitcast_fusion.2
  97.9 1.1 copy.35
  99.7 1.5 constant_dynamic-slice_fusion.3
  101.3 1.9 fusion.24
  104.1 7.4 fusion.25
  111.5 1.7 convolution_bitcast_fusion.2
  113.2 1.1 copy.35
  115.0 1.5 constant_dynamic-slice_fusion.3
  116.6 1.9 fusion.24
  119.4 7.4 fusion.25
  126.8 1.7 convolution_bitcast_fusion.2
  130.3 1.5 constant_dynamic-slice_fusion.3
  131.9 1.9 fusion.24
  134.7 7.4 fusion.25
  142.1 1.7 convolution_bitcast_fusion.2
  143.8 1.1 copy.35
  145.6 1.5 constant_dynamic-slice_fusion.3
  147.2 1.9 fusion.24
  150.0 7.4 fusion.25
  157.4 1.7 convolution_bitcast_fusion.2
  159.1 1.1 copy.35
  160.9 1.5 constant_dynamic-slice_fusion.3
  162.5 1.9 fusion.24
  165.3 7.4 fusion.25
  172.7 1.7 convolution_bitcast_fusion.2
  176.2 1.5 constant_dynamic-slice_fusion.3
  177.8 1.9 fusion.24
  180.6 7.4 fusion.25
  188.0 1.7 convolution_bitcast_fusion.2
  191.5 1.5 constant_dynamic-slice_fusion.3
  193.1 1.9 fusion.24
  195.9 7.4 fusion.25
  203.3 1.7 convolution_bitcast_fusion.2
  206.8 1.5 constant_dynamic-slice_fusion.3
  208.4 1.9 fusion.24
  211.1 7.4 fusion.25
  218.5 1.7 convolution_bitcast_fusion.2
  223.3 648.1 %all-reduce.3.cloned.1.call-done = f32[12,256,256]{2,1,0:T(8,128)} async-done(((f32[12,256,256]{2,1,0:T(8,128)}), f32[12,256,256]{2,1,0:T(8,128)}) %all-reduce.3.cloned.1.call-update) | async-done | bytes 3145744
  872.3 8.8 psum.7
  882.0 17.6 %all_to_all.18 = f32[64,1,192]{2,1,0:T(1,128)S(1)} all-to-all(f32[64,1,192]{2,1,0:T(1,128)S(1)} %reshape.21), channel_id=1, replica_groups=mesh['grp'=2,'sp'=64] {'sp'}, dimensions={0} | all-to-all | bytes 98304 | tf_op jit(solution)/shard_map/all_to_all | solution.py:55
  (76 shorter events, 35.9 us)
Async XLA Ops:
  6.5 864.9 %all-reduce.3.cloned.1.call-start = ((), (), s32[]{:S(2)}) async-start(), calls=%async_computation.1 | async-start | bytes 6291456
  7.6 7.9 collective-permute-start
  9.4 9.1 %collective-permute-start.1 = (bf16[3,8,1,16,256]{4,3,2,1,0:T(8,128)(2,1)S(1)}, bf16[3,8,1,16,256]{4,3,2,1,0:T(8,128)(2,1)S(1)}, u32[]{:S(2)}, u32[]{:S(2)}) collective-permute-start(bf16[3,8,1,16,256]{4,3,2,1,0:T(8,128)(2,1)S(1)} %get-tuple-element.101), channel_id=1, source_target_pairs={{64,0},{0,64},{65,1},{1,65},{66,2},{2,66},{67,3},{3,67},{68,4},{4,... | collective-permute-start | bytes 589832 | tf_op jit(solution)/shard_map/ppermute | solution.py:18
  15.5 13.4 %copy-start = (bf16[3,8,16,16,256]{4,3,2,1,0:T(8,128)(2,1)S(1)}, bf16[3,8,16,16,256]{4,3,2,1,0:T(8,128)(2,1)}, u32[]{:S(2)}) copy-start(bf16[3,8,16,16,256]{4,3,2,1,0:T(8,128)(2,1)} %param.4) | copy-start | bytes 9437188
  15.5 13.4 %copy-start.3 = (s32[12]{0:T(128)S(1)}, s32[12]{0:T(128)}, u32[]{:S(2)}) copy-start(s32[12]{0:T(128)} %param.5) | copy-start | bytes 148
  18.5 1.8 copy-start.1
  21.2 13.9 %collective-permute-start.2 = (bf16[3,1,18,16,256]{4,3,2,1,0:T(8,128)(2,1)}, bf16[3,1,18,16,256]{4,3,2,1,0:T(8,128)(2,1)}, u32[]{:S(2)}, u32[]{:S(2)}) collective-permute-start(bf16[3,1,18,16,256]{4,3,2,1,0:T(8,128)(2,1)} %get-tuple-element.99), channel_id=1, source_target_pairs={{0,1},{1,2},{2,3},{3,4},{4,5},{5,6},{6,7},{7,8},{8,9},{9,10},{10,1... | collective-permute-start | bytes 1327112 | tf_op jit(solution)/shard_map/ppermute | solution.py:15
  21.3 13.9 %collective-permute-start.3 = (bf16[3,1,18,16,256]{4,3,2,1,0:T(8,128)(2,1)}, bf16[3,1,18,16,256]{4,3,2,1,0:T(8,128)(2,1)}, u32[]{:S(2)}, u32[]{:S(2)}) collective-permute-start(bf16[3,1,18,16,256]{4,3,2,1,0:T(8,128)(2,1)} %get-tuple-element.100), channel_id=1, source_target_pairs={{1,0},{2,1},{3,2},{4,3},{5,4},{6,5},{7,6},{8,7},{9,8},{10,9},{11,1... | collective-permute-start | bytes 1327112 | tf_op jit(solution)/shard_map/ppermute | solution.py:18
  28.9 6.3 copy-start.2
  38.6 183.5 %copy-start.4 = (u32[128]{0:T(128)S(1)}, u32[128]{0:T(128)}, u32[]{:S(2)}) copy-start(u32[128]{0:T(128)} %constant.23) | copy-start | bytes 1540
Sparse Core Ops, SparseCore 0:
  222.2 649.1 all-reduce.2
where the time goes:
time: 912 us; the launch traced here: 910 us
  waiting for transfers between devices  655 us (72%)
  other arithmetic  93.7 us (10%)
  local copies, waits for them, and re-layouts  83.7 us (9%)
  blocking collectives  26.4 us (3%)
  matrix products  26.2 us (3%)
  between operations  14.2 us (2%)
  starting transfers between devices  9.72 us (1%)
    unnamed x2, waiting for transfers between devices  648 us
    convert_element_type x12, other arithmetic, project(): moved = moved.astype(jnp.bfloat16).reshape(-1, width)  88.8 us
    slice x24, local copies, waits for them, and re-layouts, project(): along_z = jnp.roll(centre, -1, axis=3) - jnp.roll(centre, 1, axis=3)  33.1 us
    dynamic_update_slice x24, local copies, waits for them, and re-layouts, shards(): _, stacked = lax.scan(project, jnp.zeros((), jnp.float32), velocity)  21.6 us
    dot_general x12, matrix products, project(): lax.dot_general(test_flat, moved, (((0,), (0,)), ((), ())), preferred_ele...  20.7 us
    dynamic_slice x12, local copies, waits for them, and re-layouts, shards(): _, stacked = lax.scan(project, jnp.zeros((), jnp.float32), velocity)  18.6 us
  transfers between devices with their start and end apart: 5, of which 4 were waited for; matrix products, arithmetic and copies ran while one was open for 1% of the time, Pallas kernels for 0%

commit v1 on v0

v1 whole, which is shorter than its diff:
```python
import jax
import jax.numpy as jnp
from jax import lax
from jax.experimental import pallas as pl
from jax.experimental.pallas import tpu as pltpu
from jax.sharding import Mesh, PartitionSpec as P

M = 256
NSEL = 12
HALF = NSEL // 2
CX, CY, NZ = 8, 16, 16
BLOCK = CY * NZ
SP = ("x", "yh", "z", "core")
VMEM_LIMIT = 44 * 1024 * 1024


def constants(conv, picker, shift):
    lane = lax.broadcasted_iota(jnp.int32, (1, 128), 1)
    wanted = jnp.full((1, 128), -1, jnp.int32)
    for a in range(NSEL):
        wanted = jnp.where(lane == a, conv[a], wanted)
    row = lax.broadcasted_iota(jnp.int32, (M, 128), 0)
    picker[...] = jnp.where(row == wanted, 1.0, 0.0).astype(jnp.bfloat16)
    row = lax.broadcasted_iota(jnp.int32, (BLOCK, BLOCK), 0)
    col = lax.broadcasted_iota(jnp.int32, (BLOCK, BLOCK), 1)
    base = row - row % NZ
    after = col == base + (row + 1) % NZ
    before = col == base + (row + NZ - 1) % NZ
    shift[...] = jnp.where(after, 1.0, jnp.where(before, -1.0, 0.0)).astype(jnp.bfloat16)


def prepare(rows, picker, shift, vel, dzs, mt):
    n = rows[0].shape[0]
    for c in range(3):
        vel[c, 0:n] = jnp.dot(rows[c], picker[...], preferred_element_type=jnp.float32)
        dzs[c, 0:n] = jnp.dot(shift[0:n, 0:n], rows[c], preferred_element_type=jnp.float32)
        mt[:, c * n : (c + 1) * n] = rows[c].T


def advect(ext, x, y, t, n, vel, dzs, mv):
    here = slice(t * NZ, (t + 1) * NZ)
    speeds = [vel[d, here] for d in range(3)]
    for h in range(2):
        lanes = slice(h * 128, (h + 1) * 128)
        fields = []
        for c in range(3):
            dx = ext[c, x + 1, y, :, lanes].astype(jnp.float32) - ext[c, x - 1, y, :, lanes].astype(jnp.float32)
            dy = ext[c, x, y + 1, :, lanes].astype(jnp.float32) - ext[c, x, y - 1, :, lanes].astype(jnp.float32)
            fields.append((dx, dy, dzs[c, here, lanes]))
        for a in range(NSEL):
            u, v, w = (jnp.broadcast_to(s[:, a : a + 1], (NZ, 128)) for s in speeds)
            for c, (dx, dy, dz) in enumerate(fields):
                moved = u * dx + v * dy + w * dz
                mv[a, c * n + t * NZ : c * n + (t + 1) * NZ, lanes] = moved.astype(jnp.bfloat16)


def product(a, n, mt, mv, source, acc):
    acc[a] = source[a] + jnp.dot(mt[:, 0 : 3 * n], mv[a, 0 : 3 * n], preferred_element_type=jnp.float32)


def interleave(tiles, dots):
    done = 0
    for k, tile in enumerate(tiles):
        tile()
        upto = (k + 1) * len(dots) // len(tiles)
        for dot in dots[done:upto]:
            dot()
        done = upto
    for dot in dots[done:]:
        dot()


def interior_kernel(conv, modes, acc, ext, picker, shift, vel, dzs, mt_a, mt_b, mv_a, mv_b, sems):
    copies = [pltpu.make_async_copy(modes.at[:, x], ext.at[:, x], sems.at[x]) for x in range(CX)]
    for copy in copies:
        copy.start()
    constants(conv, picker, shift)
    acc[...] = jnp.zeros_like(acc)
    blank = jnp.zeros((NSEL, NZ, M), jnp.bfloat16)
    for mv in (mv_a, mv_b):
        for c in range(3):
            mv[:, c * BLOCK : c * BLOCK + NZ] = blank
            mv[:, (c + 1) * BLOCK - NZ : (c + 1) * BLOCK] = blank
    for copy in copies:
        copy.wait()

    def stage(x, mt_w, mv_w, mt_r, mv_r):
        dots = []
        if mv_r is not None:
            dots = [lambda a=a: product(a, BLOCK, mt_r, mv_r, acc, acc) for a in range(NSEL)]
        tiles = []
        if mv_w is not None:
            rows = [ext[c, x].reshape(BLOCK, M) for c in range(3)]
            prepare(rows, picker, shift, vel, dzs, mt_w)
            tiles = [lambda y=y: advect(ext, x, y, y, BLOCK, vel, dzs, mv_w) for y in range(1, CY - 1)]
        interleave(tiles, dots)

    stage(1, mt_a, mv_a, None, None)

    def pair(j, carry):
        stage(2 * j + 2, mt_b, mv_b, mt_a, mv_a)
        stage(2 * j + 3, mt_a, mv_a, mt_b, mv_b)
        return carry

    lax.fori_loop(0, 2, pair, 0)
    stage(6, mt_b, mv_b, mt_a, mv_a)
    stage(None, None, None, mt_b, mv_b)


def boundary_kernel(conv, core, modes, near, far, yface, start, theirs, mine,
                    ext, picker, shift, vel, dzs, acc, mt_a, mt_b, mv_a, mv_b, sems):
    me = core[0]
    copies = [pltpu.make_async_copy(modes.at[:, x], ext.at[:, x + 1, 1:17], sems.at[x]) for x in range(CX)]
    copies += [
        pltpu.make_async_copy(near, ext.at[:, pl.ds(9 - 9 * me, 1), 1:17], sems.at[8]),
        pltpu.make_async_copy(far, ext.at[:, pl.ds(9 * me, 1), 1:17], sems.at[9]),
        pltpu.make_async_copy(yface.at[:, :, 0:1], ext.at[:, 1:9, 0:1], sems.at[10]),
        pltpu.make_async_copy(yface.at[:, :, 1:2], ext.at[:, 1:9, 17:18], sems.at[11]),
    ]
    for copy in copies:
        copy.start()
    constants(conv, picker, shift)
    for copy in copies:
        copy.wait()

    edge = [(x, y) for y in (1, CY) for x in range(2, CX)]
    plane = [[(x, y) for y in range(1, CY + 1)] for x in (1, CX)]
    work = [edge] + plane
    buffers = [(mt_a, mv_a), (mt_b, mv_b), (mt_a, mv_a)]
    for k in range(4):
        dots, tiles = [], []
        if k > 0:
            n_r = len(work[k - 1]) * NZ
            mt_r, mv_r = buffers[k - 1]
            source = start if k == 1 else acc
            dots = [
                lambda a=a, n_r=n_r, mt_r=mt_r, mv_r=mv_r, source=source: product(a, n_r, mt_r, mv_r, source, acc)
                for a in range(NSEL)
            ]
        if k < 3:
            n = len(work[k]) * NZ
            mt_w, mv_w = buffers[k]
            if k == 0:
                rows = [
                    jnp.concatenate([ext[c, 2:CX, y].reshape(n // 2, M) for y in (1, CY)], axis=0) for c in range(3)
                ]
            else:
                rows = [ext[c, work[k][0][0], 1 : CY + 1].reshape(n, M) for c in range(3)]
            prepare(rows, picker, shift, vel, dzs, mt_w)
            tiles = [
                lambda x=x, y=y, t=t, n=n, mv_w=mv_w: advect(ext, x, y, t, n, vel, dzs, mv_w)
                for t, (x, y) in enumerate(work[k])
            ]
        interleave(tiles, dots)

    def finish(j, carry):
        block = acc[(1 - me) * HALF + j]
        theirs[j] = (block - block.T).astype(jnp.bfloat16)
        return carry

    def keep(j, carry):
        block = acc[me * HALF + j]
        mine[j] = block - block.T
        return carry

    lax.fori_loop(0, HALF, finish, 0)
    lax.fori_loop(0, HALF, keep, 0)


SMEM = pl.BlockSpec(memory_space=pltpu.SMEM)
HBM = pl.BlockSpec(memory_space=pl.ANY)
VMEM = pl.BlockSpec(memory_space=pltpu.VMEM)
WORK = [
    pltpu.VMEM((M, 128), jnp.bfloat16),
    pltpu.VMEM((BLOCK, BLOCK), jnp.bfloat16),
    pltpu.VMEM((3, BLOCK, 128), jnp.float32),
    pltpu.VMEM((3, BLOCK, M), jnp.float32),
]
BUFFERS = [pltpu.VMEM((M, 3 * BLOCK), jnp.bfloat16)] * 2 + [pltpu.VMEM((NSEL, 3 * BLOCK, M), jnp.bfloat16)] * 2


def interior(convecting, modes):
    return pl.pallas_call(
        interior_kernel,
        out_shape=pltpu.VMEM((NSEL, M, M), jnp.float32),
        in_specs=[SMEM, HBM],
        out_specs=VMEM,
        scratch_shapes=[pltpu.VMEM((3, CX, CY, NZ, M), jnp.bfloat16)] + WORK + BUFFERS + [pltpu.SemaphoreType.DMA((CX,))],
        compiler_params=pltpu.CompilerParams(vmem_limit_bytes=VMEM_LIMIT),
        name="interior",
    )(convecting, modes)


def boundary(convecting, core, modes, near, far, yface, start):
    return pl.pallas_call(
        boundary_kernel,
        out_shape=(
            jax.ShapeDtypeStruct((HALF, M, M), jnp.bfloat16),
            jax.ShapeDtypeStruct((HALF, M, M), jnp.float32),
        ),
        in_specs=[SMEM, SMEM, HBM, HBM, HBM, HBM, VMEM],
        out_specs=(VMEM, VMEM),
        scratch_shapes=[pltpu.VMEM((3, CX + 2, CY + 2, NZ, M), jnp.bfloat16)] + WORK
        + [pltpu.VMEM((NSEL, M, M), jnp.float32)] + BUFFERS + [pltpu.SemaphoreType.DMA((12,))],
        compiler_params=pltpu.CompilerParams(vmem_limit_bytes=VMEM_LIMIT),
        name="boundary",
    )(convecting, core, modes, near, far, yface, start)


def shards(modes, convecting):
    swap = [(0, 1), (1, 0)]
    across = [(s, (s + 1) % 64 if s % 2 else (s - 1) % 64) for s in range(64)]
    core = lax.axis_index("core")
    last = (CX - 1) * core
    far = lax.ppermute(lax.dynamic_slice_in_dim(modes, last, 1, 1), SP, across)
    near = lax.ppermute(lax.dynamic_slice_in_dim(modes, CX - 1 - last, 1, 1), "core", swap)
    yface = lax.ppermute(jnp.concatenate([modes[:, :, -1:], modes[:, :, :1]], axis=2), "yl", swap)
    start = interior(convecting, modes)
    theirs, mine = boundary(convecting, core.reshape(1).astype(jnp.int32), modes, near, far, yface, start)
    paired = (mine + lax.ppermute(theirs, "core", swap).astype(jnp.float32)).astype(jnp.bfloat16)
    spread = lax.all_to_all(paired, SP, split_axis=1, concat_axis=0, tiled=True)
    owned = spread.reshape(32, NSEL, 4, M).astype(jnp.float32).sum(0)
    owned = owned + lax.ppermute(owned, "yl", swap)
    return owned * (0.25 / 512.0)


def solution(mesh):
    fine = Mesh(mesh.devices.reshape(2, 4, 2, 4, 2), ("yl",) + SP)
    placed = (P(None, SP, "yl", None, None), P())
    return jax.shard_map(
        shards, mesh=fine, in_specs=placed, out_specs=P(None, SP, None), check_vma=False
    )
```

time: 912 us -> 76.8 us (0.08)
  waiting for transfers between devices: 655 us -> 5.87 us
  other arithmetic: 93.7 us -> 1.95 us
  local copies, waits for them, and re-layouts: 83.7 us -> 3.14 us
  Pallas kernels: 0 us -> 31.5 us
  matrix products: 26.2 us -> 0 us
  between operations: 14.2 us -> 0.06 us
    unnamed x2 -> x0, waiting for transfers between devices: 648 us -> none
    convert_element_type x12 -> x1, other arithmetic: 88.8 us -> 0.29 us  [shards(): (mine + lax.ppermute(theirs, 'core', swap).astype(jnp.float32)).astype(jn...]
    slice x26 -> x1, local copies, waits for them, and re-layouts: 35.1 us -> 1.2 us  [shards(): modes[:, :, -1:]]
    pallas_call x0 -> x2, Pallas kernels: none -> 31.5 us  [the longest x1 19.4 us: interior(): pl.pallas_call(interior_kernel, out_shape=pltpu.VMEM((NSEL, M, M), jnp.fl...]
    dot_general x13 -> x0, matrix products: 26.2 us -> none  [the longest x12 20.7 us: project(): lax.dot_general(test_flat, moved, (((0,), (0,)), ((), ())), preferred_ele...]
    dynamic_update_slice x24 -> x0, local copies, waits for them, and re-layouts: 21.6 us -> none  [shards(): _, stacked = lax.scan(project, jnp.zeros((), jnp.float32), velocity)]
    dynamic_slice x12 -> x1, local copies, waits for them, and re-layouts: 18.6 us -> 1.17 us  [shards(): far = lax.ppermute(lax.dynamic_slice_in_dim(modes, last, 1, 1), SP, across)]
  transfers between devices with their start and end apart: 5 -> 5, of which waited for: 4 -> 2; matrix products, arithmetic and copies ran while one was open for 1% -> 2% of each run, Pallas kernels for 0% -> 25%
where the time goes in v1:
time: 76.8 us; the launch traced here: 76.7 us
  Pallas kernels  31.5 us (41%)
  blocking collectives  23.8 us (31%)
  starting transfers between devices  10.3 us (13%)
  waiting for transfers between devices  5.87 us (8%)
  local copies, waits for them, and re-layouts  3.14 us (4%)
  other arithmetic  1.95 us (3%)
    all_to_all x1, blocking collectives, shards(): spread = lax.all_to_all(paired, SP, split_axis=1, concat_axis=0, tiled=True)  23.8 us
    pallas_call x1, Pallas kernels, interior(): pl.pallas_call(interior_kernel, out_shape=pltpu.VMEM((NSEL, M, M), jnp.fl...  19.4 us
    pallas_call x1, Pallas kernels, boundary(): pl.pallas_call(boundary_kernel, out_shape=(jax.ShapeDtypeStruct((HALF, M,...  12.1 us
    ppermute x1, starting transfers between devices, shards(): far = lax.ppermute(lax.dynamic_slice_in_dim(modes, last, 1, 1), SP, across)  7.81 us
    ppermute x1, waiting for transfers between devices, shards(): owned = owned + lax.ppermute(owned, 'yl', swap)  3.95 us
    ppermute x1, waiting for transfers between devices, shards(): lax.ppermute(theirs, 'core', swap).astype(jnp.float32)  1.91 us
    ppermute x1, starting transfers between devices, shards(): lax.ppermute(jnp.concatenate([modes[:, :, -1:], modes[:, :, :1]], axis=2)...  1.69 us
  transfers between devices with their start and end apart: 5, of which 2 were waited for; matrix products, arithmetic and copies ran while one was open for 2% of the time, Pallas kernels for 25%

profile of v1, /device:TPU:0, one launch (start us, length us, event | category | flops | bytes accessed | tf_op | source)
XLA Modules:
  0.0 76.7 jit_solution(32569682071091270)
XLA Ops:
  0.0 0.0 copy-start
  0.0 0.0 copy-start.1
  0.0 1.2 %fusion = (bf16[3,8,1,16,256]{4,3,2,1,0:T(8,128)(2,1)S(1)}, bf16[3,8,1,16,256]{4,3,2,1,0:T(8,128)(2,1)S(1)}) fusion(bf16[3,8,16,16,256]{4,3,2,1,0:T(8,128)(2,1)} %modes.3), kind=kLoop, calls=%fused_computation.5 | loop fusion | bytes 786432 | tf_op jit(solution)/shard_map/slice | solution.py:217
  1.2 0.8 %pad_maximum_fusion = bf16[3,8,2,16,256]{4,3,2,1,0:T(8,128)(2,1)} fusion(bf16[3,8,1,16,256]{4,3,2,1,0:T(8,128)(2,1)S(1)} %get-tuple-element.10, bf16[3,8,1,16,256]{4,3,2,1,0:T(8,128)(2,1)S(1)} %get-tuple-element.9), kind=kLoop, calls=%fused_computation.1 | loop fusion | flops 196608 | bytes 786432 | tf_op jit(solution)/shard_map/concatenate | solution.py:217
  2.0 1.7 %collective-permute-start.2 = (bf16[3,8,2,16,256]{4,3,2,1,0:T(8,128)(2,1)}, bf16[3,8,2,16,256]{4,3,2,1,0:T(8,128)(2,1)S(1)}, u32[]{:S(2)}, u32[]{:S(2)}) collective-permute-start(bf16[3,8,2,16,256]{4,3,2,1,0:T(8,128)(2,1)} %pad_maximum_fusion), channel_id=1, source_target_pairs={{0,64},{64,0},{1,65},{65,1},{2,66},{66,2},{3,67},{67,3},{4,68},{68... | collective-permute-start | bytes 1179656 | tf_op jit(solution)/shard_map/ppermute | solution.py:217
  3.7 1.2 %constant_dynamic-slice_fusion = (bf16[3,1,16,16,256]{4,3,2,1,0:T(8,128)(2,1)S(1)}, bf16[3,1,16,16,256]{4,3,2,1,0:T(8,128)(2,1)S(1)}) fusion(bf16[3,8,16,16,256]{4,3,2,1,0:T(8,128)(2,1)} %modes.3, s32[]{:T(128)S(6)} %select_n.7, s32[]{:T(128)S(6)} %select_n.6), kind=kLoop, calls=%fused_computation.3 | loop fusion | bytes 1572872 | tf_op jit(solution)/shard_map/dynamic_slice | solution.py:215
  4.8 7.8 %collective-permute-start.1 = (bf16[3,1,16,16,256]{4,3,2,1,0:T(8,128)(2,1)S(1)}, bf16[3,1,16,16,256]{4,3,2,1,0:T(8,128)(2,1)S(1)}, u32[]{:S(2)}, u32[]{:S(2)}) collective-permute-start(bf16[3,1,16,16,256]{4,3,2,1,0:T(8,128)(2,1)S(1)} %get-tuple-element.11), channel_id=1, source_target_pairs={{0,63},{1,2},{2,1},{3,4},{4,3},{5,6},{6,5},{7,8},{8,7},{9,10},{10,... | collective-permute-start | bytes 1179656 | tf_op jit(solution)/shard_map/ppermute | solution.py:215
  12.7 0.0 collective-permute-start
  12.7 0.0 copy-done
  12.7 0.0 copy-done.1
  12.7 19.4 %interior.1.start = f32[12,256,256]{2,1,0:T(8,128)S(1)} custom-call(s32[12]{0:T(128)S(1)} %copy-done.1, bf16[3,8,16,16,256]{4,3,2,1,0:T(8,128)(2,1)S(1)} %copy-done), custom_call_target="tpu_custom_call" | custom-call | tf_op jit(solution)/shard_map/interior/pallas_call | solution.py:183
  32.1 0.0 collective-permute-done.2.yface
  32.1 0.0 collective-permute-done.1.far
  32.1 0.0 collective-permute-done.near
  32.2 12.1 %boundary.1 = (bf16[6,256,256]{2,1,0:T(8,128)(2,1)S(1)}, f32[6,256,256]{2,1,0:T(8,128)S(1)}) custom-call(s32[12]{0:T(128)S(1)} %copy-done.1, s32[1]{0:T(128)} %bitcast.core, bf16[3,8,16,16,256]{4,3,2,1,0:T(8,128)(2,1)S(1)} %copy-done, bf16[3,1,16,16,256]{4,3,2,1,0:T(8,128)(2,1)S(1)} %collective-permute-done.near, ...), custom_call_target="tpu_custom_call" | custom-call | tf_op jit(solution)/shard_map/boundary/pallas_call | solution.py:195
  44.2 0.6 collective-permute-start.3
  44.8 1.9 %collective-permute-done.3 = bf16[6,256,256]{2,1,0:T(8,128)(2,1)S(1)} collective-permute-done((bf16[6,256,256]{2,1,0:T(8,128)(2,1)S(1)}, bf16[6,256,256]{2,1,0:T(8,128)(2,1)S(1)}, u32[]{:S(2)}, u32[]{:S(2)}) %collective-permute-start.3) | collective-permute-done | bytes 786464 | tf_op jit(solution)/shard_map/ppermute | solution.py:220
  46.7 0.3 add_convert_fusion
  47.0 0.5 copy.4
  47.5 23.8 %all_to_all.4 = bf16[6,256,256]{2,0,1:T(8,128)(2,1)S(1)} all-to-all(bf16[6,256,256]{2,0,1:T(8,128)(2,1)S(1)} %copy.4), channel_id=1, replica_groups=mesh['yl'=2,'x'=4,'yh'=2,'z'=4,'core'=2] {'x','yh','z','core'}, dimensions={1} | all-to-all | bytes 1572864 | tf_op jit(solution)/shard_map/all_to_all | solution.py:221
  71.3 0.3 copy.5
  71.6 0.2 reduce_sum.9
  71.9 0.2 collective-permute-start.4
  72.1 4.0 %collective-permute-done.4 = f32[12,4,256]{2,1,0:T(4,128)S(1)} collective-permute-done((f32[12,4,256]{2,1,0:T(4,128)S(1)}, f32[12,4,256]{2,1,0:T(4,128)S(1)}, u32[]{:S(2)}, u32[]{:S(2)}) %collective-permute-start.4) | collective-permute-done | bytes 49184 | tf_op jit(solution)/shard_map/ppermute | solution.py:223
  76.0 0.6 add_multiply_fusion
Async XLA Ops:
  0.0 12.7 %copy-start = (bf16[3,8,16,16,256]{4,3,2,1,0:T(8,128)(2,1)S(1)}, bf16[3,8,16,16,256]{4,3,2,1,0:T(8,128)(2,1)}, u32[]{:S(2)}) copy-start(bf16[3,8,16,16,256]{4,3,2,1,0:T(8,128)(2,1)} %modes.3) | copy-start | bytes 9437188
  0.0 12.7 %copy-start.1 = (s32[12]{0:T(128)S(1)}, s32[12]{0:T(128)}, u32[]{:S(2)}) copy-start(s32[12]{0:T(128)} %conv.3) | copy-start | bytes 148
  2.0 30.1 %collective-permute-start.2 = (bf16[3,8,2,16,256]{4,3,2,1,0:T(8,128)(2,1)}, bf16[3,8,2,16,256]{4,3,2,1,0:T(8,128)(2,1)S(1)}, u32[]{:S(2)}, u32[]{:S(2)}) collective-permute-start(bf16[3,8,2,16,256]{4,3,2,1,0:T(8,128)(2,1)} %pad_maximum_fusion), channel_id=1, source_target_pairs={{0,64},{64,0},{1,65},{65,1},{2,66},{66,2},{3,67},{67,3},{4,68},{68... | collective-permute-start | bytes 1179656 | tf_op jit(solution)/shard_map/ppermute | solution.py:217
  4.8 27.3 %collective-permute-start.1 = (bf16[3,1,16,16,256]{4,3,2,1,0:T(8,128)(2,1)S(1)}, bf16[3,1,16,16,256]{4,3,2,1,0:T(8,128)(2,1)S(1)}, u32[]{:S(2)}, u32[]{:S(2)}) collective-permute-start(bf16[3,1,16,16,256]{4,3,2,1,0:T(8,128)(2,1)S(1)} %get-tuple-element.11), channel_id=1, source_target_pairs={{0,63},{1,2},{2,1},{3,4},{4,3},{5,6},{6,5},{7,8},{8,7},{9,10},{10,... | collective-permute-start | bytes 1179656 | tf_op jit(solution)/shard_map/ppermute | solution.py:215
  12.7 19.5 %collective-permute-start = (bf16[3,1,16,16,256]{4,3,2,1,0:T(8,128)(2,1)S(1)}, bf16[3,1,16,16,256]{4,3,2,1,0:T(8,128)(2,1)S(1)}, u32[]{:S(2)}, u32[]{:S(2)}) collective-permute-start(bf16[3,1,16,16,256]{4,3,2,1,0:T(8,128)(2,1)S(1)} %get-tuple-element.12), channel_id=1, source_target_pairs={{0,1},{1,0},{2,3},{3,2},{4,5},{5,4},{6,7},{7,6},{8,9},{9,8},{10,11... | collective-permute-start | bytes 1179656 | tf_op jit(solution)/shard_map/ppermute | solution.py:216
  44.2 2.5 %collective-permute-start.3 = (bf16[6,256,256]{2,1,0:T(8,128)(2,1)S(1)}, bf16[6,256,256]{2,1,0:T(8,128)(2,1)S(1)}, u32[]{:S(2)}, u32[]{:S(2)}) collective-permute-start(bf16[6,256,256]{2,1,0:T(8,128)(2,1)S(1)} %get-tuple-element.8), channel_id=1, source_target_pairs={{0,1},{1,0},{2,3},{3,2},{4,5},{5,4},{6,7},{7,6},{8,9},{9,8},{10,11... | collective-permute-start | bytes 2359304 | tf_op jit(solution)/shard_map/ppermute | solution.py:220
  71.9 4.2 %collective-permute-start.4 = (f32[12,4,256]{2,1,0:T(4,128)S(1)}, f32[12,4,256]{2,1,0:T(4,128)S(1)}, u32[]{:S(2)}, u32[]{:S(2)}) collective-permute-start(f32[12,4,256]{2,1,0:T(4,128)S(1)} %reduce_sum.9), channel_id=1, source_target_pairs={{0,64},{64,0},{1,65},{65,1},{2,66},{66,2},{3,67},{67,3},{4,68},{68... | collective-permute-start | bytes 147464 | tf_op jit(solution)/shard_map/ppermute | solution.py:223

commit v2 on v1

v2 whole, which is shorter than its diff:
```python
import jax
import jax.numpy as jnp
from jax import lax
from jax.experimental import pallas as pl
from jax.experimental.pallas import tpu as pltpu
from jax.sharding import Mesh, PartitionSpec as P

M = 256
NSEL = 12
HALF = NSEL // 2
GROUP = 4
CX, CY, NZ = 8, 16, 16
BLOCK = CY * NZ
SP = ("x", "yh", "z", "core")
VMEM_LIMIT = 44 * 1024 * 1024


def constants(conv, picker, shift):
    lane = lax.broadcasted_iota(jnp.int32, (1, 128), 1)
    wanted = jnp.full((1, 128), -1, jnp.int32)
    for a in range(NSEL):
        wanted = jnp.where(lane == a, conv[a], wanted)
    row = lax.broadcasted_iota(jnp.int32, (M, 128), 0)
    picker[...] = jnp.where(row == wanted, 1.0, 0.0).astype(jnp.bfloat16)
    row = lax.broadcasted_iota(jnp.int32, (BLOCK, BLOCK), 0)
    col = lax.broadcasted_iota(jnp.int32, (BLOCK, BLOCK), 1)
    base = row - row % NZ
    after = col == base + (row + 1) % NZ
    before = col == base + (row + NZ - 1) % NZ
    shift[...] = jnp.where(after, 1.0, jnp.where(before, -1.0, 0.0)).astype(jnp.bfloat16)


def prepare(rows, picker, shift, vel, fld, mt):
    n = rows[0].shape[0]
    for c in range(3):
        vel[c, 0:n] = jnp.dot(rows[c], picker[...], preferred_element_type=jnp.float32)
        fld[2, c, 0:n] = jnp.dot(shift[0:n, 0:n], rows[c], preferred_element_type=jnp.float32)
        mt[:, c * n : (c + 1) * n] = rows[c].T


def difference(at, x, y, t, fld):
    here = slice(t * NZ, (t + 1) * NZ)
    for c in range(3):
        fld[0, c, here] = at(c, x + 1, y).astype(jnp.float32) - at(c, x - 1, y).astype(jnp.float32)
        fld[1, c, here] = at(c, x, y + 1).astype(jnp.float32) - at(c, x, y - 1).astype(jnp.float32)


def advect(t, n, vel, fld, mv, group):
    here = slice(t * NZ, (t + 1) * NZ)
    chosen = range(group * GROUP, (group + 1) * GROUP)
    speeds = [vel[d, here] for d in range(3)]
    wide = [[jnp.broadcast_to(s[:, a : a + 1], (NZ, 128)) for s in speeds] for a in chosen]
    for c in range(3):
        for h in range(2):
            lanes = slice(h * 128, (h + 1) * 128)
            dx, dy, dz = (fld[d, c, here, lanes] for d in range(3))
            for a, (u, v, w) in zip(chosen, wide):
                moved = u * dx + v * dy + w * dz
                mv[a, c * n + t * NZ : c * n + (t + 1) * NZ, lanes] = moved.astype(jnp.bfloat16)


def product(a, n, mt, mv, source, acc):
    acc[a] = source[a] + jnp.dot(mt[:, 0 : 3 * n], mv[a, 0 : 3 * n], preferred_element_type=jnp.float32)


def interleave(items, dots):
    done = 0
    for k, item in enumerate(items):
        item()
        upto = (k + 1) * len(dots) // len(items)
        for dot in dots[done:upto]:
            dot()
        done = upto
    for dot in dots[done:]:
        dot()


def works(at, tiles, n, vel, fld, mv):
    items = []
    for t, (x, y) in tiles:
        items.append(lambda x=x, y=y, t=t: difference(at, x, y, t, fld))
    for t, _ in tiles:
        for group in range(NSEL // GROUP):
            items.append(lambda t=t, group=group: advect(t, n, vel, fld, mv, group))
    return items


def interior_kernel(conv, modes, acc, picker, shift, vel, fld, mt_a, mt_b, mv_a, mv_b):
    constants(conv, picker, shift)
    acc[...] = jnp.zeros_like(acc)
    blank = jnp.zeros((NSEL, NZ, M), jnp.bfloat16)
    for mv in (mv_a, mv_b):
        for c in range(3):
            mv[:, c * BLOCK : c * BLOCK + NZ] = blank
            mv[:, (c + 1) * BLOCK - NZ : (c + 1) * BLOCK] = blank

    def at(c, x, y):
        return modes[c, x, y]

    def stage(x, mt_w, mv_w, mt_r, mv_r):
        dots = []
        if mv_r is not None:
            dots = [lambda a=a: product(a, BLOCK, mt_r, mv_r, acc, acc) for a in range(NSEL)]
        items = []
        if mv_w is not None:
            prepare([modes[c, x].reshape(BLOCK, M) for c in range(3)], picker, shift, vel, fld, mt_w)
            items = works(at, [(y, (x, y)) for y in range(1, CY - 1)], BLOCK, vel, fld, mv_w)
        interleave(items, dots)

    stage(1, mt_a, mv_a, None, None)

    def pair(j, carry):
        stage(2 * j + 2, mt_b, mv_b, mt_a, mv_a)
        stage(2 * j + 3, mt_a, mv_a, mt_b, mv_b)
        return carry

    lax.fori_loop(0, 2, pair, 0)
    stage(6, mt_b, mv_b, mt_a, mv_a)
    stage(None, None, None, mt_b, mv_b)


def boundary_kernel(conv, core, modes, near, far, yface, start, theirs, mine,
                    xface, picker, shift, vel, fld, acc, mt_a, mt_b, mv_a, mv_b):
    me = core[0]
    constants(conv, picker, shift)
    xface[:, pl.ds(1 - me, 1)] = near[...]
    xface[:, pl.ds(me, 1)] = far[...]

    def at(c, x, y):
        if x in (-1, CX):
            return xface[c, 1 if x == CX else 0, y]
        if y in (-1, CY):
            return yface[c, x, 1 if y == CY else 0]
        return modes[c, x, y]

    edge = [(x, y) for y in (0, CY - 1) for x in range(1, CX - 1)]
    plane = [[(x, y) for y in range(CY)] for x in (0, CX - 1)]
    work = [edge] + plane
    buffers = [(mt_a, mv_a), (mt_b, mv_b), (mt_a, mv_a)]
    for k in range(4):
        dots, items = [], []
        if k > 0:
            n_r = len(work[k - 1]) * NZ
            mt_r, mv_r = buffers[k - 1]
            source = start if k == 1 else acc
            dots = [
                lambda a=a, n_r=n_r, mt_r=mt_r, mv_r=mv_r, source=source: product(a, n_r, mt_r, mv_r, source, acc)
                for a in range(NSEL)
            ]
        if k < 3:
            n = len(work[k]) * NZ
            mt_w, mv_w = buffers[k]
            if k == 0:
                rows = [
                    jnp.concatenate([modes[c, 1 : CX - 1, y].reshape(n // 2, M) for y in (0, CY - 1)], axis=0)
                    for c in range(3)
                ]
            else:
                rows = [modes[c, work[k][0][0]].reshape(n, M) for c in range(3)]
            prepare(rows, picker, shift, vel, fld, mt_w)
            items = works(at, list(enumerate(work[k])), n, vel, fld, mv_w)
        interleave(items, dots)

    def finish(j, carry):
        block = acc[(1 - me) * HALF + j]
        theirs[j] = (block - block.T).astype(jnp.bfloat16)
        return carry

    def keep(j, carry):
        block = acc[me * HALF + j]
        mine[j] = block - block.T
        return carry

    lax.fori_loop(0, HALF, finish, 0)
    lax.fori_loop(0, HALF, keep, 0)


def faces_kernel(core, modes, near, far, yface, sems):
    last = (CX - 1) * core[0]
    copies = [
        pltpu.make_async_copy(modes.at[:, pl.ds(last, 1)], far, sems.at[0]),
        pltpu.make_async_copy(modes.at[:, pl.ds(CX - 1 - last, 1)], near, sems.at[1]),
        pltpu.make_async_copy(modes.at[:, :, CY - 1 : CY], yface.at[:, :, 0:1], sems.at[2]),
        pltpu.make_async_copy(modes.at[:, :, 0:1], yface.at[:, :, 1:2], sems.at[3]),
    ]
    for copy in copies:
        copy.start()
    for copy in copies:
        copy.wait()


SMEM = pl.BlockSpec(memory_space=pltpu.SMEM)
HBM = pl.BlockSpec(memory_space=pl.ANY)
VMEM = pl.BlockSpec(memory_space=pltpu.VMEM)
WORK = [
    pltpu.VMEM((M, 128), jnp.bfloat16),
    pltpu.VMEM((BLOCK, BLOCK), jnp.bfloat16),
    pltpu.VMEM((3, BLOCK, 128), jnp.float32),
    pltpu.VMEM((3, 3, BLOCK, M), jnp.float32),
]
BUFFERS = [pltpu.VMEM((M, 3 * BLOCK), jnp.bfloat16)] * 2 + [pltpu.VMEM((NSEL, 3 * BLOCK, M), jnp.bfloat16)] * 2


def faces(core, modes):
    return pl.pallas_call(
        faces_kernel,
        out_shape=(
            pltpu.VMEM((3, 1, CY, NZ, M), jnp.bfloat16),
            pltpu.VMEM((3, 1, CY, NZ, M), jnp.bfloat16),
            pltpu.VMEM((3, CX, 2, NZ, M), jnp.bfloat16),
        ),
        in_specs=[SMEM, HBM],
        out_specs=(VMEM, VMEM, VMEM),
        scratch_shapes=[pltpu.SemaphoreType.DMA((4,))],
        compiler_params=pltpu.CompilerParams(vmem_limit_bytes=VMEM_LIMIT),
        name="faces",
    )(core, modes)


def interior(convecting, modes):
    return pl.pallas_call(
        interior_kernel,
        out_shape=pltpu.VMEM((NSEL, M, M), jnp.float32),
        in_specs=[SMEM, VMEM],
        out_specs=VMEM,
        scratch_shapes=WORK + BUFFERS,
        compiler_params=pltpu.CompilerParams(vmem_limit_bytes=VMEM_LIMIT),
        name="interior",
    )(convecting, modes)


def boundary(convecting, core, modes, near, far, yface, start):
    return pl.pallas_call(
        boundary_kernel,
        out_shape=(pltpu.VMEM((HALF, M, M), jnp.bfloat16), pltpu.VMEM((HALF, M, M), jnp.float32)),
        in_specs=[SMEM, SMEM] + [VMEM] * 5,
        out_specs=(VMEM, VMEM),
        scratch_shapes=[pltpu.VMEM((3, 2, CY, NZ, M), jnp.bfloat16)] + WORK
        + [pltpu.VMEM((NSEL, M, M), jnp.float32)] + BUFFERS,
        compiler_params=pltpu.CompilerParams(vmem_limit_bytes=VMEM_LIMIT),
        name="boundary",
    )(convecting, core, modes, near, far, yface, start)


def shards(modes, convecting):
    swap = [(0, 1), (1, 0)]
    across = [(s, (s + 1) % 64 if s % 2 else (s - 1) % 64) for s in range(64)]
    core = lax.axis_index("core").reshape(1).astype(jnp.int32)
    near, far, yface = faces(core, modes)
    far = lax.ppermute(far, SP, across)
    near = lax.ppermute(near, "core", swap)
    yface = lax.ppermute(yface, "yl", swap)
    start = interior(convecting, modes)
    theirs, mine = boundary(convecting, core, modes, near, far, yface, start)
    paired = (mine + lax.ppermute(theirs, "core", swap).astype(jnp.float32)).astype(jnp.bfloat16)
    spread = lax.all_to_all(paired, SP, split_axis=1, concat_axis=0, tiled=True)
    owned = spread.reshape(32, NSEL, 4, M).astype(jnp.float32).sum(0)
    owned = owned + lax.ppermute(owned, "yl", swap)
    return owned * (0.25 / 512.0)


def solution(mesh):
    fine = Mesh(mesh.devices.reshape(2, 4, 2, 4, 2), ("yl",) + SP)
    placed = (P(None, SP, "yl", None, None), P())
    return jax.shard_map(
        shards, mesh=fine, in_specs=placed, out_specs=P(None, SP, None), check_vma=False
    )
```

time: 76.8 us -> 76.5 us (level)
  Pallas kernels: 31.5 us -> 32.8 us
  other arithmetic: 1.95 us -> 1.13 us
    unnamed x4 -> x6, local copies, waits for them, and re-layouts: 0.01 us -> 1.9 us
    pallas_call x1, Pallas kernels: 19.4 us -> 20.9 us  [interior(): pl.pallas_call(interior_kernel, out_shape=pltpu.VMEM((NSEL, M, M), jnp.fl...]
    slice x1 -> x0, local copies, waits for them, and re-layouts: 1.2 us -> none  [shards(): modes[:, :, -1:]]
    dynamic_slice x1 -> x0, local copies, waits for them, and re-layouts: 1.17 us -> none  [shards(): far = lax.ppermute(lax.dynamic_slice_in_dim(modes, last, 1, 1), SP, across)]
    ppermute x1, waiting for transfers between devices: 3.95 us -> 3.11 us  [shards(): owned = owned + lax.ppermute(owned, 'yl', swap)]
    ppermute x1, starting transfers between devices: 0.21 us -> 1.06 us  [shards(): owned = owned + lax.ppermute(owned, 'yl', swap)]
    concatenate x1 -> x0, other arithmetic: 0.78 us -> none  [shards(): jnp.concatenate([modes[:, :, -1:], modes[:, :, :1]], axis=2)]
    pallas_call x1 -> x2, Pallas kernels: 12.1 us -> 11.9 us  [the longest x1 11.7 us: boundary(): pl.pallas_call(boundary_kernel, out_shape=(pltpu.VMEM((HALF, M, M), jnp.b...]
  transfers between devices with their start and end apart: 5 -> 5, of which waited for: 2 -> 2; matrix products, arithmetic and copies ran while one was open for 2% -> 0% of each run, Pallas kernels for 25% -> 27%
where the time goes in v2:
time: 76.5 us; the launch traced here: 76.3 us
  Pallas kernels  32.8 us (43%)
  blocking collectives  23.4 us (31%)
  starting transfers between devices  11 us (14%)
  waiting for transfers between devices  5.39 us (7%)
  local copies, waits for them, and re-layouts  2.66 us (3%)
  other arithmetic  1.13 us (1%)
    all_to_all x1, blocking collectives, shards(): spread = lax.all_to_all(paired, SP, split_axis=1, concat_axis=0, tiled=True)  23.4 us
    pallas_call x1, Pallas kernels, interior(): pl.pallas_call(interior_kernel, out_shape=pltpu.VMEM((NSEL, M, M), jnp.fl...  20.9 us
    pallas_call x1, Pallas kernels, boundary(): pl.pallas_call(boundary_kernel, out_shape=(pltpu.VMEM((HALF, M, M), jnp.b...  11.7 us
    ppermute x1, starting transfers between devices, shards(): far = lax.ppermute(far, SP, across)  9.08 us
    ppermute x1, waiting for transfers between devices, shards(): owned = owned + lax.ppermute(owned, 'yl', swap)  3.11 us
    ppermute x1, waiting for transfers between devices, shards(): lax.ppermute(theirs, 'core', swap).astype(jnp.float32)  2.27 us
    unnamed x6, local copies, waits for them, and re-layouts  1.9 us
  transfers between devices with their start and end apart: 5, of which 2 were waited for; matrix products, arithmetic and copies ran while one was open for 0% of the time, Pallas kernels for 27%

profile of v2, /device:TPU:0, one launch (start us, length us, event | category | flops | bytes accessed | tf_op | source)
XLA Modules:
  0.0 76.3 jit_solution(1546716807113102804)
XLA Ops:
  0.0 0.0 copy-start
  0.0 1.9 %copy-done = bf16[3,8,16,16,256]{4,3,2,1,0:T(8,128)(2,1)S(1)} copy-done((bf16[3,8,16,16,256]{4,3,2,1,0:T(8,128)(2,1)S(1)}, bf16[3,8,16,16,256]{4,3,2,1,0:T(8,128)(2,1)}, u32[]{:S(2)}) %copy-start) | copy-done | bytes 3145752
  1.9 0.0 copy-start.1
  1.9 0.0 copy-start.2
  1.9 0.2 faces.1
  2.1 0.1 collective-permute-start
  2.2 9.1 %collective-permute-start.1 = (bf16[3,1,16,16,256]{4,3,2,1,0:T(8,128)(2,1)S(1)}, bf16[3,1,16,16,256]{4,3,2,1,0:T(8,128)(2,1)S(1)}, u32[]{:S(2)}, u32[]{:S(2)}) collective-permute-start(bf16[3,1,16,16,256]{4,3,2,1,0:T(8,128)(2,1)S(1)} %get-tuple-element.11), channel_id=1, source_target_pairs={{0,63},{1,2},{2,1},{3,4},{4,3},{5,6},{6,5},{7,8},{8,7},{9,10},{10,... | collective-permute-start | bytes 1179656 | tf_op jit(solution)/shard_map/ppermute | solution.py:250
  11.3 0.7 collective-permute-start.2
  12.0 0.0 copy-done.1
  12.0 0.0 copy-done.2
  12.0 20.9 %interior.1.start = f32[12,256,256]{2,1,0:T(8,128)S(1)} custom-call(s32[12]{0:T(128)S(1)} %copy-done.2, bf16[3,8,16,16,256]{4,3,2,1,0:T(8,128)(2,1)S(1)} %copy-done.1), custom_call_target="tpu_custom_call" | custom-call | tf_op jit(solution)/shard_map/interior/pallas_call | solution.py:221
  32.9 0.0 collective-permute-done.near
  32.9 0.0 collective-permute-done.1.far
  32.9 0.0 collective-permute-done.2.yface
  32.9 11.7 %boundary.1 = (bf16[6,256,256]{2,1,0:T(8,128)(2,1)S(1)}, f32[6,256,256]{2,1,0:T(8,128)S(1)}) custom-call(s32[12]{0:T(128)S(1)} %copy-done.2, s32[1]{0:T(128)} %bitcast.core, bf16[3,8,16,16,256]{4,3,2,1,0:T(8,128)(2,1)S(1)} %copy-done.1, bf16[3,1,16,16,256]{4,3,2,1,0:T(8,128)(2,1)S(1)} %collective-permute-done.near, ...), custom_call_target="tpu_custom_call" | custom-call | tf_op jit(solution)/shard_map/boundary/pallas_call | solution.py:233
  44.6 0.1 collective-permute-start.3
  44.7 2.3 %collective-permute-done.3 = bf16[6,256,256]{2,1,0:T(8,128)(2,1)S(1)} collective-permute-done((bf16[6,256,256]{2,1,0:T(8,128)(2,1)S(1)}, bf16[6,256,256]{2,1,0:T(8,128)(2,1)S(1)}, u32[]{:S(2)}, u32[]{:S(2)}) %collective-permute-start.3) | collective-permute-done | bytes 786464 | tf_op jit(solution)/shard_map/ppermute | solution.py:255
  46.9 0.3 add_convert_fusion
  47.2 0.5 copy.4
  47.6 23.4 %all_to_all.4 = bf16[6,256,256]{2,0,1:T(8,128)(2,1)S(1)} all-to-all(bf16[6,256,256]{2,0,1:T(8,128)(2,1)S(1)} %copy.4), channel_id=1, replica_groups=mesh['yl'=2,'x'=4,'yh'=2,'z'=4,'core'=2] {'x','yh','z','core'}, dimensions={1} | all-to-all | bytes 1572864 | tf_op jit(solution)/shard_map/all_to_all | solution.py:256
  71.0 0.3 copy.5
  71.3 0.2 reduce_sum.9
  71.5 1.1 %collective-permute-start.4 = (f32[12,4,256]{2,1,0:T(4,128)S(1)}, f32[12,4,256]{2,1,0:T(4,128)S(1)}, u32[]{:S(2)}, u32[]{:S(2)}) collective-permute-start(f32[12,4,256]{2,1,0:T(4,128)S(1)} %reduce_sum.9), channel_id=1, source_target_pairs={{0,64},{64,0},{1,65},{65,1},{2,66},{66,2},{3,67},{67,3},{4,68},{68... | collective-permute-start | bytes 147464 | tf_op jit(solution)/shard_map/ppermute | solution.py:258
  72.6 3.1 %collective-permute-done.4 = f32[12,4,256]{2,1,0:T(4,128)S(1)} collective-permute-done((f32[12,4,256]{2,1,0:T(4,128)S(1)}, f32[12,4,256]{2,1,0:T(4,128)S(1)}, u32[]{:S(2)}, u32[]{:S(2)}) %collective-permute-start.4) | collective-permute-done | bytes 49184 | tf_op jit(solution)/shard_map/ppermute | solution.py:258
  75.7 0.6 add_multiply_fusion
Async XLA Ops:
  0.0 1.9 %copy-start = (bf16[3,8,16,16,256]{4,3,2,1,0:T(8,128)(2,1)S(1)}, bf16[3,8,16,16,256]{4,3,2,1,0:T(8,128)(2,1)}, u32[]{:S(2)}) copy-start(bf16[3,8,16,16,256]{4,3,2,1,0:T(8,128)(2,1)} %modes.5) | copy-start | bytes 9437188
  1.9 10.1 %copy-start.1 = (bf16[3,8,16,16,256]{4,3,2,1,0:T(8,128)(2,1)S(1)}, bf16[3,8,16,16,256]{4,3,2,1,0:T(8,128)(2,1)}, u32[]{:S(2)}) copy-start(bf16[3,8,16,16,256]{4,3,2,1,0:T(8,128)(2,1)} %modes.5) | copy-start | bytes 9437188
  1.9 10.1 %copy-start.2 = (s32[12]{0:T(128)S(1)}, s32[12]{0:T(128)}, u32[]{:S(2)}) copy-start(s32[12]{0:T(128)} %conv.3) | copy-start | bytes 148
  2.1 30.7 %collective-permute-start = (bf16[3,1,16,16,256]{4,3,2,1,0:T(8,128)(2,1)S(1)}, bf16[3,1,16,16,256]{4,3,2,1,0:T(8,128)(2,1)S(1)}, u32[]{:S(2)}, u32[]{:S(2)}) collective-permute-start(bf16[3,1,16,16,256]{4,3,2,1,0:T(8,128)(2,1)S(1)} %get-tuple-element.10), channel_id=1, source_target_pairs={{0,1},{1,0},{2,3},{3,2},{4,5},{5,4},{6,7},{7,6},{8,9},{9,8},{10,11... | collective-permute-start | bytes 1179656 | tf_op jit(solution)/shard_map/ppermute | solution.py:251
  2.2 30.6 %collective-permute-start.1 = (bf16[3,1,16,16,256]{4,3,2,1,0:T(8,128)(2,1)S(1)}, bf16[3,1,16,16,256]{4,3,2,1,0:T(8,128)(2,1)S(1)}, u32[]{:S(2)}, u32[]{:S(2)}) collective-permute-start(bf16[3,1,16,16,256]{4,3,2,1,0:T(8,128)(2,1)S(1)} %get-tuple-element.11), channel_id=1, source_target_pairs={{0,63},{1,2},{2,1},{3,4},{4,3},{5,6},{6,5},{7,8},{8,7},{9,10},{10,... | collective-permute-start | bytes 1179656 | tf_op jit(solution)/shard_map/ppermute | solution.py:250
  11.3 21.6 %collective-permute-start.2 = (bf16[3,8,2,16,256]{4,3,2,1,0:T(8,128)(2,1)S(1)}, bf16[3,8,2,16,256]{4,3,2,1,0:T(8,128)(2,1)S(1)}, u32[]{:S(2)}, u32[]{:S(2)}) collective-permute-start(bf16[3,8,2,16,256]{4,3,2,1,0:T(8,128)(2,1)S(1)} %get-tuple-element.12), channel_id=1, source_target_pairs={{0,64},{64,0},{1,65},{65,1},{2,66},{66,2},{3,67},{67,3},{4,68},{68... | collective-permute-start | bytes 1179656 | tf_op jit(solution)/shard_map/ppermute | solution.py:252
  44.6 2.4 %collective-permute-start.3 = (bf16[6,256,256]{2,1,0:T(8,128)(2,1)S(1)}, bf16[6,256,256]{2,1,0:T(8,128)(2,1)S(1)}, u32[]{:S(2)}, u32[]{:S(2)}) collective-permute-start(bf16[6,256,256]{2,1,0:T(8,128)(2,1)S(1)} %get-tuple-element.14), channel_id=1, source_target_pairs={{0,1},{1,0},{2,3},{3,2},{4,5},{5,4},{6,7},{7,6},{8,9},{9,8},{10,11... | collective-permute-start | bytes 2359304 | tf_op jit(solution)/shard_map/ppermute | solution.py:255
  71.5 4.2 %collective-permute-start.4 = (f32[12,4,256]{2,1,0:T(4,128)S(1)}, f32[12,4,256]{2,1,0:T(4,128)S(1)}, u32[]{:S(2)}, u32[]{:S(2)}) collective-permute-start(f32[12,4,256]{2,1,0:T(4,128)S(1)} %reduce_sum.9), channel_id=1, source_target_pairs={{0,64},{64,0},{1,65},{65,1},{2,66},{66,2},{3,67},{67,3},{4,68},{68... | collective-permute-start | bytes 147464 | tf_op jit(solution)/shard_map/ppermute | solution.py:258

commit v3 on v2

v3 whole, which is shorter than its diff:
```python
import jax
import jax.numpy as jnp
from jax import lax
from jax.experimental import pallas as pl
from jax.experimental.pallas import tpu as pltpu
from jax.sharding import Mesh, PartitionSpec as P

M = 256
NSEL = 12
CX, CY, NZ = 8, 16, 16
BLOCK = CY * NZ
SP = ("x", "yh", "z", "core")
VMEM_LIMIT = 44 * 1024 * 1024


def constants(conv, picker, shift):
    lane = lax.broadcasted_iota(jnp.int32, (1, 128), 1)
    wanted = jnp.full((1, 128), -1, jnp.int32)
    for a in range(NSEL):
        wanted = jnp.where(lane == a, conv[a], wanted)
    row = lax.broadcasted_iota(jnp.int32, (M, 128), 0)
    picker[...] = jnp.where(row == wanted, 1.0, 0.0).astype(jnp.bfloat16)
    row = lax.broadcasted_iota(jnp.int32, (BLOCK, BLOCK), 0)
    col = lax.broadcasted_iota(jnp.int32, (BLOCK, BLOCK), 1)
    base = row - row % NZ
    after = col == base + (row + 1) % NZ
    before = col == base + (row + NZ - 1) % NZ
    shift[...] = jnp.where(after, 1.0, jnp.where(before, -1.0, 0.0)).astype(jnp.bfloat16)


def survey(rows, picker, shift, vel, dz):
    n = rows[0].shape[0]
    for c in range(3):
        vel[c, 0:n] = jnp.dot(rows[c], picker[...], preferred_element_type=jnp.float32)
        dz[c, 0:n] = jnp.dot(shift[0:n, 0:n], rows[c], preferred_element_type=jnp.float32)


def transpose(rows, mt):
    n = rows[0].shape[0]
    for c in range(3):
        mt[:, c * n : (c + 1) * n] = rows[c].T


def advect(at, x, y, t, n, vel, dzs, mv):
    here = slice(t * NZ, (t + 1) * NZ)
    speeds = [vel[d, here] for d in range(3)]
    for h in range(2):
        lanes = slice(h * 128, (h + 1) * 128)
        fields = []
        for c in range(3):
            dx = at(c, x + 1, y, lanes).astype(jnp.float32) - at(c, x - 1, y, lanes).astype(jnp.float32)
            dy = at(c, x, y + 1, lanes).astype(jnp.float32) - at(c, x, y - 1, lanes).astype(jnp.float32)
            fields.append((dx, dy, dzs[c, here, lanes]))
        for a in range(NSEL):
            u, v, w = (jnp.broadcast_to(s[:, a : a + 1], (NZ, 128)) for s in speeds)
            for c, (dx, dy, dz) in enumerate(fields):
                moved = u * dx + v * dy + w * dz
                mv[a, c * n + t * NZ : c * n + (t + 1) * NZ, lanes] = moved.astype(jnp.bfloat16)


def product(a, n, mt, mv, source, acc):
    block = jnp.dot(mt[:, 0 : 3 * n], mv[a, 0 : 3 * n], preferred_element_type=jnp.float32)
    acc[a] = block if source is None else source[a] + block


def interleave(items, dots):
    done = 0
    for k, item in enumerate(items):
        item()
        upto = (k + 1) * len(dots) // len(items)
        for dot in dots[done:upto]:
            dot()
        done = upto
    for dot in dots[done:]:
        dot()


def works(at, tiles, n, vel, dz, mv):
    return [lambda x=x, y=y, t=t: advect(at, x, y, t, n, vel, dz, mv) for t, (x, y) in tiles]


def interior_kernel(conv, modes, acc, picker, shift, vel_a, vel_b, dz_a, dz_b, mt_a, mt_b, mv_a, mv_b):
    constants(conv, picker, shift)
    blank = jnp.zeros((NSEL, NZ, M), jnp.bfloat16)
    for mv in (mv_a, mv_b):
        for c in range(3):
            mv[:, c * BLOCK : c * BLOCK + NZ] = blank
            mv[:, (c + 1) * BLOCK - NZ : (c + 1) * BLOCK] = blank
    sets = [(vel_a, dz_a, mt_a, mv_a), (vel_b, dz_b, mt_b, mv_b)]

    def at(c, x, y, lanes):
        return modes[c, x, y, :, lanes]

    def plane(x):
        return [modes[c, x].reshape(BLOCK, M) for c in range(3)]

    def stage(x, side, dots=True, first=False, last=False):
        vel, dz, mt, mv = sets[side]
        vel_n, dz_n, mt_r, mv_r = sets[1 - side]
        todo = []
        if dots:
            source = None if first else acc
            todo = [lambda a=a: product(a, BLOCK, mt_r, mv_r, source, acc) for a in range(NSEL)]
        items = works(at, [(y, (x, y)) for y in range(1, CY - 1)], BLOCK, vel, dz, mv)
        items.insert(len(items) // 3, lambda: transpose(plane(x), mt))
        if not last:
            items.insert(2 * len(items) // 3, lambda: survey(plane(x + 1), picker, shift, vel_n, dz_n))
        interleave(items, todo)

    survey(plane(1), picker, shift, vel_a, dz_a)
    stage(1, 0, dots=False)
    stage(2, 1, first=True)

    def pair(j, carry):
        stage(2 * j + 3, 0)
        stage(2 * j + 4, 1)
        return carry

    lax.fori_loop(0, 2, pair, 0)
    for a in range(NSEL):
        product(a, BLOCK, mt_b, mv_b, acc, acc)


def boundary_kernel(conv, core, modes, near, far, yface, start, theirs, mine,
                    xface, acc, picker, shift, vel_a, vel_b, dz_a, dz_b, mt_a, mt_b, mv_a, mv_b):
    me = core[0]
    constants(conv, picker, shift)
    xface[:, pl.ds(1 - me, 1)] = near[...]
    xface[:, pl.ds(me, 1)] = far[...]
    sets = [(vel_a, dz_a, mt_a, mv_a), (vel_b, dz_b, mt_b, mv_b)]

    def at(c, x, y, lanes):
        if x in (-1, CX):
            return xface[c, 1 if x == CX else 0, y, :, lanes]
        if y in (-1, CY):
            return yface[c, x, 1 if y == CY else 0, :, lanes]
        return modes[c, x, y, :, lanes]

    edge = [(x, y) for y in (0, CY - 1) for x in range(1, CX - 1)]
    work = [edge] + [[(x, y) for y in range(CY)] for x in (0, CX - 1)]

    def rows(k):
        if k == 0:
            half = len(edge) * NZ // 2
            return [
                jnp.concatenate([modes[c, 1 : CX - 1, y].reshape(half, M) for y in (0, CY - 1)], axis=0)
                for c in range(3)
            ]
        return [modes[c, work[k][0][0]].reshape(BLOCK, M) for c in range(3)]

    survey(rows(0), picker, shift, vel_a, dz_a)
    for k in range(3):
        vel, dz, mt, mv = sets[k % 2]
        vel_n, dz_n, mt_r, mv_r = sets[(k + 1) % 2]
        n = len(work[k]) * NZ
        todo = []
        if k > 0:
            before = len(work[k - 1]) * NZ
            source = start if k == 1 else acc
            todo = [lambda a=a: product(a, before, mt_r, mv_r, source, acc) for a in range(NSEL)]
        items = works(at, list(enumerate(work[k])), n, vel, dz, mv)
        items.insert(len(items) // 3, lambda: transpose(rows(k), mt))
        if k < 2:
            items.insert(2 * len(items) // 3, lambda: survey(rows(k + 1), picker, shift, vel_n, dz_n))
        interleave(items, todo)
    for a in range(NSEL):
        product(a, BLOCK, mt_a, mv_a, acc, acc)

    def finish(a, carry):
        block = acc[a]
        block = (block - block.T).reshape(M // 8, 2, 4, M)
        theirs[a] = jnp.where(me == 0, block[:, 1], block[:, 0]).astype(jnp.bfloat16)
        mine[a] = jnp.where(me == 0, block[:, 0], block[:, 1])
        return carry

    lax.fori_loop(0, NSEL, finish, 0)


def faces_kernel(core, modes, near, far, yface, sems):
    last = (CX - 1) * core[0]
    copies = [
        pltpu.make_async_copy(modes.at[:, pl.ds(last, 1)], far, sems.at[0]),
        pltpu.make_async_copy(modes.at[:, pl.ds(CX - 1 - last, 1)], near, sems.at[1]),
        pltpu.make_async_copy(modes.at[:, :, CY - 1 : CY], yface.at[:, :, 0:1], sems.at[2]),
        pltpu.make_async_copy(modes.at[:, :, 0:1], yface.at[:, :, 1:2], sems.at[3]),
    ]
    for copy in copies:
        copy.start()
    for copy in copies:
        copy.wait()


SMEM = pl.BlockSpec(memory_space=pltpu.SMEM)
HBM = pl.BlockSpec(memory_space=pltpu.HBM)
VMEM = pl.BlockSpec(memory_space=pltpu.VMEM)
WORK = (
    [pltpu.VMEM((M, 128), jnp.bfloat16), pltpu.VMEM((BLOCK, BLOCK), jnp.bfloat16)]
    + [pltpu.VMEM((3, BLOCK, 128), jnp.float32)] * 2
    + [pltpu.VMEM((3, BLOCK, M), jnp.float32)] * 2
)
BUFFERS = [pltpu.VMEM((M, 3 * BLOCK), jnp.bfloat16)] * 2 + [pltpu.VMEM((NSEL, 3 * BLOCK, M), jnp.bfloat16)] * 2


def faces(core, modes):
    return pl.pallas_call(
        faces_kernel,
        out_shape=(
            pltpu.VMEM((3, 1, CY, NZ, M), jnp.bfloat16),
            pltpu.VMEM((3, 1, CY, NZ, M), jnp.bfloat16),
            pltpu.VMEM((3, CX, 2, NZ, M), jnp.bfloat16),
        ),
        in_specs=[SMEM, HBM],
        out_specs=(VMEM, VMEM, VMEM),
        scratch_shapes=[pltpu.SemaphoreType.DMA((4,))],
        compiler_params=pltpu.CompilerParams(vmem_limit_bytes=VMEM_LIMIT),
        name="faces",
    )(core, modes)


def interior(convecting, modes):
    return pl.pallas_call(
        interior_kernel,
        out_shape=pltpu.VMEM((NSEL, M, M), jnp.float32),
        in_specs=[SMEM, VMEM],
        out_specs=VMEM,
        scratch_shapes=WORK + BUFFERS,
        compiler_params=pltpu.CompilerParams(vmem_limit_bytes=VMEM_LIMIT),
        name="interior",
    )(convecting, modes)


def boundary(convecting, core, modes, near, far, yface, start):
    return pl.pallas_call(
        boundary_kernel,
        out_shape=(
            pltpu.VMEM((NSEL, M // 8, 4, M), jnp.bfloat16),
            pltpu.VMEM((NSEL, M // 8, 4, M), jnp.float32),
        ),
        in_specs=[SMEM, SMEM] + [VMEM] * 5,
        out_specs=(VMEM, VMEM),
        scratch_shapes=[pltpu.VMEM((3, 2, CY, NZ, M), jnp.bfloat16), pltpu.VMEM((NSEL, M, M), jnp.float32)]
        + WORK + BUFFERS,
        compiler_params=pltpu.CompilerParams(vmem_limit_bytes=VMEM_LIMIT),
        name="boundary",
    )(convecting, core, modes, near, far, yface, start)


def shards(modes, convecting):
    swap = [(0, 1), (1, 0)]
    across = [(s, (s + 1) % 64 if s % 2 else (s - 1) % 64) for s in range(64)]
    core = lax.axis_index("core").reshape(1).astype(jnp.int32)
    near, far, yface = faces(core, modes)
    far = lax.ppermute(far, SP, across)
    near = lax.ppermute(near, "core", swap)
    yface = lax.ppermute(yface, "yl", swap)
    start = interior(convecting, modes)
    theirs, mine = boundary(convecting, core, modes, near, far, yface, start)
    paired = (mine + lax.ppermute(theirs, "core", swap).astype(jnp.float32)).astype(jnp.bfloat16)
    spread = lax.all_to_all(paired, SP[:3], split_axis=1, concat_axis=0, tiled=True)
    owned = spread.reshape(32, NSEL, 4, M).astype(jnp.float32).sum(0)
    owned = owned + lax.ppermute(owned, "yl", swap)
    return owned * (0.25 / 512.0)


def solution(mesh):
    fine = Mesh(mesh.devices.reshape(2, 4, 2, 4, 2), ("yl",) + SP)
    placed = (P(None, SP, "yl", None, None), P())
    return jax.shard_map(
        shards, mesh=fine, in_specs=placed, out_specs=P(None, SP, None), check_vma=False
    )
```

time: 76.5 us -> 71.2 us (0.931)
  blocking collectives: 23.4 us -> 19.3 us
  Pallas kernels: 32.8 us -> 31.6 us
    all_to_all x1, blocking collectives: 23.4 us -> 19.3 us  [shards(): lax.all_to_all(paired, SP[:3], split_axis=1, concat_axis=0, tiled=True)]
    pallas_call x1, Pallas kernels: 20.9 us -> 19.8 us  [interior(): pl.pallas_call(interior_kernel, out_shape=pltpu.VMEM((NSEL, M, M), jnp.fl...]
  transfers between devices with their start and end apart: 5 -> 5, of which waited for: 2 -> 2; matrix products, arithmetic and copies ran while one was open for 0% -> 0% of each run, Pallas kernels for 27% -> 28%
where the time goes in v3:
time: 71.2 us; the launch traced here: 71 us
  Pallas kernels  31.6 us (44%)
  blocking collectives  19.3 us (27%)
  starting transfers between devices  10.8 us (15%)
  waiting for transfers between devices  5.53 us (8%)
  local copies, waits for them, and re-layouts  2.17 us (3%)
  other arithmetic  1.45 us (2%)
    pallas_call x1, Pallas kernels, interior(): pl.pallas_call(interior_kernel, out_shape=pltpu.VMEM((NSEL, M, M), jnp.fl...  19.8 us
    all_to_all x1, blocking collectives, shards(): lax.all_to_all(paired, SP[:3], split_axis=1, concat_axis=0, tiled=True)  19.3 us
    pallas_call x1, Pallas kernels, boundary(): pl.pallas_call(boundary_kernel, out_shape=(pltpu.VMEM((NSEL, M // 8, 4, M...  11.5 us
    ppermute x1, starting transfers between devices, shards(): far = lax.ppermute(far, SP, across)  9.08 us
    ppermute x1, waiting for transfers between devices, shards(): owned = owned + lax.ppermute(owned, 'yl', swap)  3.25 us
    ppermute x1, waiting for transfers between devices, shards(): lax.ppermute(theirs, 'core', swap).astype(jnp.float32)  2.27 us
    unnamed x6, local copies, waits for them, and re-layouts  1.9 us
  transfers between devices with their start and end apart: 5, of which 2 were waited for; matrix products, arithmetic and copies ran while one was open for 0% of the time, Pallas kernels for 28%

profile of v3, /device:TPU:0, one launch (start us, length us, event | category | flops | bytes accessed | tf_op | source)
XLA Modules:
  0.0 71.0 jit_solution(14628719788971861801)
XLA Ops:
  0.0 0.0 copy-start
  0.0 1.9 %copy-done = bf16[3,8,16,16,256]{4,3,2,1,0:T(8,128)(2,1)S(1)} copy-done((bf16[3,8,16,16,256]{4,3,2,1,0:T(8,128)(2,1)S(1)}, bf16[3,8,16,16,256]{4,3,2,1,0:T(8,128)(2,1)}, u32[]{:S(2)}) %copy-start) | copy-done | bytes 3145752
  1.9 0.0 copy-start.1
  1.9 0.0 copy-start.2
  1.9 0.2 faces.1
  2.1 0.1 collective-permute-start
  2.2 9.1 %collective-permute-start.1 = (bf16[3,1,16,16,256]{4,3,2,1,0:T(8,128)(2,1)S(1)}, bf16[3,1,16,16,256]{4,3,2,1,0:T(8,128)(2,1)S(1)}, u32[]{:S(2)}, u32[]{:S(2)}) collective-permute-start(bf16[3,1,16,16,256]{4,3,2,1,0:T(8,128)(2,1)S(1)} %get-tuple-element.11), channel_id=1, source_target_pairs={{0,63},{1,2},{2,1},{3,4},{4,3},{5,6},{6,5},{7,8},{8,7},{9,10},{10,... | collective-permute-start | bytes 1179656 | tf_op jit(solution)/shard_map/ppermute | solution.py:253
  11.3 0.7 collective-permute-start.2
  12.0 0.0 copy-done.1
  12.0 0.0 copy-done.2
  12.0 19.8 %interior.1.start = f32[12,256,256]{2,1,0:T(8,128)S(1)} custom-call(s32[12]{0:T(128)S(1)} %copy-done.2, bf16[3,8,16,16,256]{4,3,2,1,0:T(8,128)(2,1)S(1)} %copy-done.1), custom_call_target="tpu_custom_call" | custom-call | tf_op jit(solution)/shard_map/interior/pallas_call | solution.py:221
  31.8 0.0 collective-permute-done.near
  31.8 0.0 collective-permute-done.1.far
  31.9 0.0 collective-permute-done.2.yface
  31.9 11.5 %boundary.1 = (bf16[12,32,4,256]{3,2,1,0:T(4,128)(2,1)S(1)}, f32[12,32,4,256]{3,2,1,0:T(4,128)S(1)}) custom-call(s32[12]{0:T(128)S(1)} %copy-done.2, s32[1]{0:T(128)} %bitcast.core, bf16[3,8,16,16,256]{4,3,2,1,0:T(8,128)(2,1)S(1)} %copy-done.1, bf16[3,1,16,16,256]{4,3,2,1,0:T(8,128)(2,1)S(1)} %collective-permute-done.near, ...), custom_call_target="tpu_custom_call" | custom-call | tf_op jit(solution)/shard_map/boundary/pallas_call | solution.py:233
  43.4 0.1 collective-permute-start.3
  43.5 2.3 %collective-permute-done.3 = bf16[12,32,4,256]{3,2,1,0:T(4,128)(2,1)S(1)} collective-permute-done((bf16[12,32,4,256]{3,2,1,0:T(4,128)(2,1)S(1)}, bf16[12,32,4,256]{3,2,1,0:T(4,128)(2,1)S(1)}, u32[]{:S(2)}, u32[]{:S(2)}) %collective-permute-start.3) | collective-permute-done | bytes 786464 | tf_op jit(solution)/shard_map/ppermute | solution.py:258
  45.8 0.5 add_convert_fusion
  46.2 0.3 copy.3
  46.5 19.3 %all_to_all.4 = bf16[12,32,4,256]{3,2,0,1:T(4,128)(2,1)S(1)} all-to-all(bf16[12,32,4,256]{3,2,0,1:T(4,128)(2,1)S(1)} %copy.3), channel_id=1, replica_groups=mesh['yl'=2,'x'=4,'yh'=2,'z'=4,'core'=2] {'x','yh','z'}, dimensions={1} | all-to-all | bytes 1572864 | tf_op jit(solution)/shard_map/all_to_all | solution.py:259
  65.9 0.3 convert_reduce_fusion
  66.2 0.9 %collective-permute-start.4 = (f32[12,4,256]{2,1,0:T(4,128)S(1)}, f32[12,4,256]{2,1,0:T(4,128)S(1)}, u32[]{:S(2)}, u32[]{:S(2)}) collective-permute-start(f32[12,4,256]{2,1,0:T(4,128)S(1)} %convert_reduce_fusion), channel_id=1, source_target_pairs={{0,64},{64,0},{1,65},{65,1},{2,66},{66,2},{3,67},{67,3},{4,68},{68... | collective-permute-start | bytes 147464 | tf_op jit(solution)/shard_map/ppermute | solution.py:261
  67.1 3.3 %collective-permute-done.4 = f32[12,4,256]{2,1,0:T(4,128)S(1)} collective-permute-done((f32[12,4,256]{2,1,0:T(4,128)S(1)}, f32[12,4,256]{2,1,0:T(4,128)S(1)}, u32[]{:S(2)}, u32[]{:S(2)}) %collective-permute-start.4) | collective-permute-done | bytes 49184 | tf_op jit(solution)/shard_map/ppermute | solution.py:261
  70.4 0.6 add_multiply_fusion
Async XLA Ops:
  0.0 1.9 %copy-start = (bf16[3,8,16,16,256]{4,3,2,1,0:T(8,128)(2,1)S(1)}, bf16[3,8,16,16,256]{4,3,2,1,0:T(8,128)(2,1)}, u32[]{:S(2)}) copy-start(bf16[3,8,16,16,256]{4,3,2,1,0:T(8,128)(2,1)} %modes.5) | copy-start | bytes 9437188
  1.9 10.1 %copy-start.1 = (bf16[3,8,16,16,256]{4,3,2,1,0:T(8,128)(2,1)S(1)}, bf16[3,8,16,16,256]{4,3,2,1,0:T(8,128)(2,1)}, u32[]{:S(2)}) copy-start(bf16[3,8,16,16,256]{4,3,2,1,0:T(8,128)(2,1)} %modes.5) | copy-start | bytes 9437188
  1.9 10.1 %copy-start.2 = (s32[12]{0:T(128)S(1)}, s32[12]{0:T(128)}, u32[]{:S(2)}) copy-start(s32[12]{0:T(128)} %conv.3) | copy-start | bytes 148
  2.1 29.7 %collective-permute-start = (bf16[3,1,16,16,256]{4,3,2,1,0:T(8,128)(2,1)S(1)}, bf16[3,1,16,16,256]{4,3,2,1,0:T(8,128)(2,1)S(1)}, u32[]{:S(2)}, u32[]{:S(2)}) collective-permute-start(bf16[3,1,16,16,256]{4,3,2,1,0:T(8,128)(2,1)S(1)} %get-tuple-element.10), channel_id=1, source_target_pairs={{0,1},{1,0},{2,3},{3,2},{4,5},{5,4},{6,7},{7,6},{8,9},{9,8},{10,11... | collective-permute-start | bytes 1179656 | tf_op jit(solution)/shard_map/ppermute | solution.py:254
  2.2 29.6 %collective-permute-start.1 = (bf16[3,1,16,16,256]{4,3,2,1,0:T(8,128)(2,1)S(1)}, bf16[3,1,16,16,256]{4,3,2,1,0:T(8,128)(2,1)S(1)}, u32[]{:S(2)}, u32[]{:S(2)}) collective-permute-start(bf16[3,1,16,16,256]{4,3,2,1,0:T(8,128)(2,1)S(1)} %get-tuple-element.11), channel_id=1, source_target_pairs={{0,63},{1,2},{2,1},{3,4},{4,3},{5,6},{6,5},{7,8},{8,7},{9,10},{10,... | collective-permute-start | bytes 1179656 | tf_op jit(solution)/shard_map/ppermute | solution.py:253
  11.3 20.6 %collective-permute-start.2 = (bf16[3,8,2,16,256]{4,3,2,1,0:T(8,128)(2,1)S(1)}, bf16[3,8,2,16,256]{4,3,2,1,0:T(8,128)(2,1)S(1)}, u32[]{:S(2)}, u32[]{:S(2)}) collective-permute-start(bf16[3,8,2,16,256]{4,3,2,1,0:T(8,128)(2,1)S(1)} %get-tuple-element.12), channel_id=1, source_target_pairs={{0,64},{64,0},{1,65},{65,1},{2,66},{66,2},{3,67},{67,3},{4,68},{68... | collective-permute-start | bytes 1179656 | tf_op jit(solution)/shard_map/ppermute | solution.py:255
  43.4 2.4 %collective-permute-start.3 = (bf16[12,32,4,256]{3,2,1,0:T(4,128)(2,1)S(1)}, bf16[12,32,4,256]{3,2,1,0:T(4,128)(2,1)S(1)}, u32[]{:S(2)}, u32[]{:S(2)}) collective-permute-start(bf16[12,32,4,256]{3,2,1,0:T(4,128)(2,1)S(1)} %get-tuple-element.14), channel_id=1, source_target_pairs={{0,1},{1,0},{2,3},{3,2},{4,5},{5,4},{6,7},{7,6},{8,9},{9,8},{10,11... | collective-permute-start | bytes 2359304 | tf_op jit(solution)/shard_map/ppermute | solution.py:258
  66.2 4.2 %collective-permute-start.4 = (f32[12,4,256]{2,1,0:T(4,128)S(1)}, f32[12,4,256]{2,1,0:T(4,128)S(1)}, u32[]{:S(2)}, u32[]{:S(2)}) collective-permute-start(f32[12,4,256]{2,1,0:T(4,128)S(1)} %convert_reduce_fusion), channel_id=1, source_target_pairs={{0,64},{64,0},{1,65},{65,1},{2,66},{66,2},{3,67},{67,3},{4,68},{68... | collective-permute-start | bytes 147464 | tf_op jit(solution)/shard_map/ppermute | solution.py:261
